TPU v7x, 256 devices: a whole 4x4x8 slice. The times are simulated.
256 devices in a mesh: shard: 64 (over y, z, core), tensor: 4 (over x).
Axes of the slice: x: 4, y: 4, z: 8, core: 2. Of those that a mesh axis runs over, the one named last changes fastest.
Arguments:
- gradient: bfloat16 [64, 1024, 1024], P(None, 'shard', 'tensor'), may hold values from -64 to 64, as said below
- momentum: float32 [64, 1024, 1024], P(None, 'shard', 'tensor'), may hold values from -64 to 64, as said below
Outputs:
- momentum_out: float32 [64, 1024, 1024], P(None, 'shard', 'tensor')
- update: float32 [64, 1024, 1024], P(None, 'shard', 'tensor')
Inputs may be any that keep to these rules, and one draw needn't show every extreme that they name: `gradient`: finite real values. `momentum`: finite real values.
All inputs are finite; a program needn't handle non-finite values.
Results may differ from a plain program's by a relative error of at most 0.0003.
Values sent between devices are 32-bit elements; how exact they have to be, the bound alone decides.
No kernel may reach another device: no remote copies, remote signals or barrier semaphores. Data moves between devices by JAX's collectives and lax.ppermute only.
A program may use at most 64 MiB of HBM per device.

v0:
```python
import math
import jax
import jax.numpy as jnp
from jax import lax
from jax.sharding import PartitionSpec as P

D = 1024
BLOCK = 1024
ITERS = 3
first_coef = 3.4445
second_coef = -4.775
third_coef = 2.0315
decay_rate = 0.95


def product(left, right):
    return jnp.einsum(
        "ij,jl->il",
        left,
        right,
        precision=lax.Precision.HIGHEST,
        preferred_element_type=jnp.float32,
    )


def against(left, right):
    return jnp.einsum(
        "ij,lj->il",
        left,
        right,
        precision=lax.Precision.HIGHEST,
        preferred_element_type=jnp.float32,
    )


def per_device(gradient, momentum):
    widened = gradient.astype(jnp.float32)
    momentum_out = decay_rate * momentum + widened
    direction = widened + decay_rate * momentum_out
    by_owner = lax.all_to_all(direction, "shard", split_axis=0, concat_axis=0, tiled=True)
    row_pieces = lax.all_to_all(by_owner, "tensor", split_axis=1, concat_axis=2, tiled=True)
    piece_count = row_pieces.shape[0]
    piece_rows = row_pieces.shape[1]
    width = row_pieces.shape[2]
    iterate = row_pieces.reshape(piece_count * piece_rows, width)
    norm_total = lax.psum(jnp.sum(iterate * iterate), "tensor")
    iterate = iterate / (jnp.sqrt(norm_total) + 1e-07)
    for sweep_index in range(ITERS):
        full_rows = lax.all_gather(iterate, "tensor", axis=0, tiled=True)
        gram_rows = against(iterate, full_rows)
        full_gram = lax.all_gather(gram_rows, "tensor", axis=0, tiled=True)
        square_rows = product(gram_rows, full_gram)
        polynomial = second_coef * gram_rows + third_coef * square_rows
        iterate = first_coef * iterate + product(polynomial, full_rows)
    result = (0.2 * math.sqrt(max(BLOCK, D)) * iterate).reshape(piece_count, piece_rows, width)
    update = lax.all_to_all(
        lax.all_to_all(result, "shard", split_axis=0, concat_axis=0, tiled=True),
        "tensor",
        split_axis=2,
        concat_axis=1,
        tiled=True,
    )
    return (momentum_out, update)


def solution(mesh):
    placed = (P(None, "shard", "tensor"), P(None, "shard", "tensor"))
    return jax.shard_map(
        per_device,
        mesh=mesh,
        in_specs=placed,
        out_specs=(P(None, "shard", "tensor"), P(None, "shard", "tensor")),
        check_vma=False,
    )
```

profile of v0, /device:TPU:1, one launch (start us, length us, event | category | flops | bytes accessed | tf_op | source)
XLA Modules:
  0.0 516.5 jit_solution(14466420875342971486)
XLA Ops:
  7.2 0.0 all-gather.7.cloned.1.call-start
  7.2 2.6 convert_add_fusion
  9.8 41.5 %all_to_all.37 = f32[64,16,256]{2,1,0:T(8,128)S(1)} all-to-all(f32[64,16,256]{2,1,0:T(8,128)S(1)} %get-tuple-element.4), channel_id=1, replica_groups=mesh['shard'=64,'tensor'=4] {'shard'}, dimensions={0} | all-to-all | bytes 2097152 | tf_op jit(solution)/shard_map/all_to_all | solution.py:40
  51.2 0.6 copy.12
  51.8 18.7 %all_to_all.38 = f32[64,16,256]{2,0,1:T(8,128)S(1)} all-to-all(f32[64,16,256]{2,0,1:T(8,128)S(1)} %copy.12), channel_id=1, replica_groups=mesh['shard'=64,'tensor'=4] {'tensor'}, dimensions={1} | all-to-all | bytes 2097152 | tf_op jit(solution)/shard_map/all_to_all | solution.py:41
  70.5 0.9 multiply_reduce_fusion
  71.4 7.6 %psum.7 = f32[]{:T(128)} all-reduce(f32[]{:T(128)} %multiply_reduce_fusion), channel_id=1, replica_groups=mesh['shard'=64,'tensor'=4] {'tensor'}, use_global_device_ids=true, to_apply=%region_1.0 | all-reduce | flops 1 | bytes 8 | tf_op jit(solution)/shard_map/psum | solution.py:46
  79.6 0.1 broadcast_divide_fusion
  79.7 0.7 copy.13
  80.4 1.2 copy.16
  81.6 0.0 all-gather.7.cloned.1.call-update
  81.6 0.0 all-gather.9.cloned.1.call-start
  81.6 47.9 %all-gather.7.cloned.1.call-done = f32[1024,1024]{1,0:T(8,128)} async-done(((f32[256,1024]{1,0:T(8,128)}), f32[1024,1024]{1,0:T(8,128)}) %all-gather.7.cloned.1.call-update) | async-done | bytes 4194320 | tf_op jit(solution)/shard_map/all_gather | solution.py:49
  129.6 7.3 %fusion.4 = f32[256,1024]{1,0:T(8,128)} fusion(f32[256,1024]{1,0:T(8,128)} %bitcast.29, f32[1024,1024]{1,0:T(8,128)} %all-gather.7.cloned.1.call-done), kind=kOutput, calls=%fused_computation.14 | convolution fusion | flops 3221225472 | bytes 6291456 | tf_op jit(solution)/shard_map/ij,lj->il/dot_general | solution.py:27
  136.8 0.0 copy-start.5
  136.8 0.0 all-gather.9.cloned.1.call-update
  136.9 0.3 all-gather.11.cloned.1.call-start
  137.2 50.9 %all-gather.9.cloned.1.call-done = f32[1024,1024]{1,0:T(8,128)} async-done(((f32[256,1024]{1,0:T(8,128)}), f32[1024,1024]{1,0:T(8,128)}) %all-gather.9.cloned.1.call-update) | async-done | bytes 4194320 | tf_op jit(solution)/shard_map/all_gather | solution.py:51
  188.1 0.0 copy-start
  188.1 6.7 %fusion.3 = f32[256,1024]{1,0:T(8,128)S(1)} fusion(f32[256,1024]{1,0:T(8,128)} %fusion.4, f32[1024,1024]{1,0:T(8,128)} %all-gather.9.cloned.1.call-done), kind=kOutput, calls=%fused_computation.9 | convolution fusion | flops 3222011904 | bytes 6291456 | tf_op jit(solution)/shard_map/ij,jl->il/dot_general | solution.py:17
  194.8 0.0 copy-done.5
  194.8 0.0 copy-done
  194.8 4.7 convolution_add_fusion.2
  199.5 0.0 all-gather.11.cloned.1.call-update
  199.6 0.0 all-gather.13.cloned.1.call-start
  199.6 51.2 %all-gather.11.cloned.1.call-done = f32[1024,1024]{1,0:T(8,128)} async-done(((f32[256,1024]{1,0:T(8,128)}), f32[1024,1024]{1,0:T(8,128)}) %all-gather.11.cloned.1.call-update) | async-done | bytes 4194320 | tf_op jit(solution)/shard_map/all_gather | solution.py:49
  250.8 7.3 %fusion.5 = f32[256,1024]{1,0:T(8,128)} fusion(f32[256,1024]{1,0:T(8,128)} %convolution_add_fusion.2, f32[1024,1024]{1,0:T(8,128)} %all-gather.11.cloned.1.call-done), kind=kOutput, calls=%fused_computation.15 | convolution fusion | flops 3221225472 | bytes 6291456 | tf_op jit(solution)/shard_map/ij,lj->il/dot_general | solution.py:27
  258.1 0.0 copy-start.3
  258.1 0.0 all-gather.13.cloned.1.call-update
  258.1 0.6 all-gather.15.cloned.1.call-start
  258.7 50.7 %all-gather.13.cloned.1.call-done = f32[1024,1024]{1,0:T(8,128)} async-done(((f32[256,1024]{1,0:T(8,128)}), f32[1024,1024]{1,0:T(8,128)}) %all-gather.13.cloned.1.call-update) | async-done | bytes 4194320 | tf_op jit(solution)/shard_map/all_gather | solution.py:51
  309.4 0.0 copy-start.1
  309.4 6.7 %fusion.2 = f32[256,1024]{1,0:T(8,128)S(1)} fusion(f32[256,1024]{1,0:T(8,128)} %fusion.5, f32[1024,1024]{1,0:T(8,128)} %all-gather.13.cloned.1.call-done), kind=kOutput, calls=%fused_computation.6 | convolution fusion | flops 3222011904 | bytes 6291456 | tf_op jit(solution)/shard_map/ij,jl->il/dot_general | solution.py:17
  316.1 0.0 copy-done.3
  316.1 0.0 copy-done.1
  316.1 4.7 convolution_add_fusion.1
  320.8 0.0 all-gather.15.cloned.1.call-update
  320.8 0.2 all-gather.17.cloned.1.call-start
  321.0 51.0 %all-gather.15.cloned.1.call-done = f32[1024,1024]{1,0:T(8,128)} async-done(((f32[256,1024]{1,0:T(8,128)}), f32[1024,1024]{1,0:T(8,128)}) %all-gather.15.cloned.1.call-update) | async-done | bytes 4194320 | tf_op jit(solution)/shard_map/all_gather | solution.py:49
  372.1 7.3 %fusion.6 = f32[256,1024]{1,0:T(8,128)} fusion(f32[256,1024]{1,0:T(8,128)} %convolution_add_fusion.1, f32[1024,1024]{1,0:T(8,128)} %all-gather.15.cloned.1.call-done), kind=kOutput, calls=%fused_computation.16 | convolution fusion | flops 3221225472 | bytes 6291456 | tf_op jit(solution)/shard_map/ij,lj->il/dot_general | solution.py:27
  379.3 0.0 copy-start.4
  379.3 0.0 all-gather.17.cloned.1.call-update
  379.4 51.3 %all-gather.17.cloned.1.call-done = f32[1024,1024]{1,0:T(8,128)} async-done(((f32[256,1024]{1,0:T(8,128)}), f32[1024,1024]{1,0:T(8,128)}) %all-gather.17.cloned.1.call-update) | async-done | bytes 4194320 | tf_op jit(solution)/shard_map/all_gather | solution.py:51
  430.6 0.0 copy-start.2
  430.6 6.7 %fusion.1 = f32[256,1024]{1,0:T(8,128)S(1)} fusion(f32[256,1024]{1,0:T(8,128)} %fusion.6, f32[1024,1024]{1,0:T(8,128)} %all-gather.17.cloned.1.call-done), kind=kOutput, calls=%fused_computation.3 | convolution fusion | flops 3222011904 | bytes 6291456 | tf_op jit(solution)/shard_map/ij,jl->il/dot_general | solution.py:17
  437.3 0.0 copy-done.4
  437.3 0.0 copy-done.2
  437.3 3.8 fusion
  441.1 0.3 reshape.14
  441.4 39.4 %all_to_all.39 = f32[64,4,1024]{2,1,0:T(4,128)S(1)} all-to-all(f32[64,4,1024]{2,1,0:T(4,128)S(1)} %reshape.14), channel_id=1, replica_groups=mesh['shard'=64,'tensor'=4] {'shard'}, dimensions={0} | all-to-all | bytes 2097152 | tf_op jit(solution)/shard_map/all_to_all | solution.py:57
  480.8 0.9 copy.14
  481.7 2.0 reshape.15
  483.8 17.7 %all_to_all.40 = f32[4,1,65536]{2,1,0:T(1,128)S(1)} all-to-all(f32[4,1,65536]{2,1,0:T(1,128)S(1)} %reshape.15), channel_id=1, replica_groups=mesh['shard'=64,'tensor'=4] {'tensor'}, dimensions={0} | all-to-all | bytes 2097152 | tf_op jit(solution)/shard_map/all_to_all | solution.py:56
  501.4 0.5 broadcast.34
  501.9 3.7 reduce.3
  505.6 1.4 reshape.16
  507.1 1.0 copy.15
  508.1 1.3 all_to_all.32
Async XLA Ops:
  7.2 122.4 %all-gather.7.cloned.1.call-start = ((), (), s32[]{:S(2)}) async-start(), calls=%async_computation.4 | async-start | bytes 5242880 | tf_op jit(solution)/shard_map/all_gather | solution.py:49
  81.6 106.5 %all-gather.9.cloned.1.call-start = ((), (), s32[]{:S(2)}) async-start(), calls=%async_computation.5 | async-start | bytes 5242880 | tf_op jit(solution)/shard_map/all_gather | solution.py:51
  136.8 58.0 %copy-start.5 = (f32[32,8,4,256]{3,1,2,0:T(8,128)S(1)}, f32[32,8,4,256]{3,1,2,0:T(8,128)}, u32[]{:S(2)}) copy-start(f32[32,8,4,256]{3,1,2,0:T(8,128)} %copy.16) | copy-start | bytes 3145732
  136.9 114.0 %all-gather.11.cloned.1.call-start = ((), (), s32[]{:S(2)}) async-start(), calls=%async_computation.6 | async-start | bytes 5242880 | tf_op jit(solution)/shard_map/all_gather | solution.py:49
  188.1 6.7 %copy-start = (f32[1024,1024]{1,0:T(8,128)S(1)}, f32[1024,1024]{1,0:T(8,128)}, u32[]{:S(2)}) copy-start(f32[1024,1024]{1,0:T(8,128)} %all-gather.7.cloned.1.call-done) | copy-start | bytes 12582916
  199.6 109.8 %all-gather.13.cloned.1.call-start = ((), (), s32[]{:S(2)}) async-start(), calls=%async_computation.7 | async-start | bytes 5242880 | tf_op jit(solution)/shard_map/all_gather | solution.py:51
  258.1 58.0 %copy-start.3 = (f32[256,1024]{1,0:T(8,128)S(1)}, f32[256,1024]{1,0:T(8,128)}, u32[]{:S(2)}) copy-start(f32[256,1024]{1,0:T(8,128)} %convolution_add_fusion.2) | copy-start | bytes 3145732
  258.1 114.0 %all-gather.15.cloned.1.call-start = ((), (), s32[]{:S(2)}) async-start(), calls=%async_computation.8 | async-start | bytes 5242880 | tf_op jit(solution)/shard_map/all_gather | solution.py:49
  309.4 6.7 %copy-start.1 = (f32[1024,1024]{1,0:T(8,128)S(1)}, f32[1024,1024]{1,0:T(8,128)}, u32[]{:S(2)}) copy-start(f32[1024,1024]{1,0:T(8,128)} %all-gather.11.cloned.1.call-done) | copy-start | bytes 12582916
  320.8 109.8 %all-gather.17.cloned.1.call-start = ((), (), s32[]{:S(2)}) async-start(), calls=%async_computation.9 | async-start | bytes 5242880 | tf_op jit(solution)/shard_map/all_gather | solution.py:51
  379.3 58.0 %copy-start.4 = (f32[256,1024]{1,0:T(8,128)S(1)}, f32[256,1024]{1,0:T(8,128)}, u32[]{:S(2)}) copy-start(f32[256,1024]{1,0:T(8,128)} %convolution_add_fusion.1) | copy-start | bytes 3145732
  430.6 6.7 %copy-start.2 = (f32[1024,1024]{1,0:T(8,128)S(1)}, f32[1024,1024]{1,0:T(8,128)}, u32[]{:S(2)}) copy-start(f32[1024,1024]{1,0:T(8,128)} %all-gather.15.cloned.1.call-done) | copy-start | bytes 12582916
Sparse Core Ops, SparseCore 0:
  81.7 47.8 all-gather.6
  137.0 51.0 all-gather.8
  199.7 51.0 all-gather.10
  258.2 51.0 all-gather.12
  320.9 51.0 all-gather.14
  379.5 51.0 all-gather.16
where the time goes:
time: 522 us; the launch traced here: 517 us
  waiting for transfers between devices  303 us (58%)
  blocking collectives  125 us (24%)
  matrix products  55 us (11%)
  between operations  15.2 us (3%)
  local copies, waits for them, and re-layouts  10 us (2%)
  other arithmetic  7.21 us (1%)
    all_gather x3, waiting for transfers between devices, per_device(): full_gram = lax.all_gather(gram_rows, 'tensor', axis=0, tiled=True)  153 us
    all_gather x3, waiting for transfers between devices, per_device(): full_rows = lax.all_gather(iterate, 'tensor', axis=0, tiled=True)  150 us
    all_to_all x1, blocking collectives, per_device(): lax.all_to_all(direction, 'shard', split_axis=0, concat_axis=0, tiled=True)  41.5 us
    all_to_all x1, blocking collectives, per_device(): lax.all_to_all(result, 'shard', split_axis=0, concat_axis=0, tiled=True)  39.4 us
    dot_general x6, matrix products, product(): jnp.einsum('ij,jl->il', left, right, precision=lax.Precision.HIGHEST, pre...  33.2 us
    dot_general x3, matrix products, against(): jnp.einsum('ij,lj->il', left, right, precision=lax.Precision.HIGHEST, pre...  21.8 us
    all_to_all x1, blocking collectives, per_device(): lax.all_to_all(by_owner, 'tensor', split_axis=1, concat_axis=2, tiled=True)  18.7 us
    all_to_all x1, blocking collectives, per_device(): lax.all_to_all(lax.all_to_all(result, 'shard', split_axis=0, concat_axis=...  17.7 us
  transfers between devices with their start and end apart: 6, of which 6 were waited for; matrix products, arithmetic and copies ran while one was open for 0% of the time, Pallas kernels for 0%

commit v1 on v0

--- a/solution.py
+++ b/solution.py
@@ -48,7 +48,10 @@
     for sweep_index in range(ITERS):
         full_rows = lax.all_gather(iterate, "tensor", axis=0, tiled=True)
         gram_rows = against(iterate, full_rows)
-        full_gram = lax.all_gather(gram_rows, "tensor", axis=0, tiled=True)
+        before = tuple((gram_rows for _ in range(jax.lax.axis_size("tensor"))))
+        e_next = jnp.stack(before)
+        finding = jax.lax.all_to_all(e_next, axis_name="tensor", split_axis=0, concat_axis=0)
+        full_gram = jnp.concatenate(finding, 0)
         square_rows = product(gram_rows, full_gram)
         polynomial = second_coef * gram_rows + third_coef * square_rows
         iterate = first_coef * iterate + product(polynomial, full_rows)

time: 522 us -> 510 us (0.977)
  blocking collectives: 125 us -> 278 us
  waiting for transfers between devices: 303 us -> 151 us
  matrix products: 55 us -> 42.4 us
    all_gather x3 -> x0, waiting for transfers between devices: 153 us -> none  [per_device(): full_gram = lax.all_gather(gram_rows, 'tensor', axis=0, tiled=True)]
    all_to_all x0 -> x3, blocking collectives: none -> 153 us  [per_device(): jax.lax.all_to_all(e_next, axis_name='tensor', split_axis=0, concat_axis=0)]
    dot_general x6, matrix products: 33.2 us -> 24.6 us  [product(): jnp.einsum('ij,jl->il', left, right, precision=lax.Precision.HIGHEST, pre...]
  transfers between devices with their start and end apart: 6 -> 3, of which waited for: 6 -> 3; matrix products, arithmetic and copies ran while one was open for 0% -> 0% of each run, Pallas kernels for 0% -> 0%
where the time goes in v1:
time: 510 us; the launch traced here: 505 us
  blocking collectives  278 us (55%)
  waiting for transfers between devices  151 us (30%)
  matrix products  42.4 us (8%)
  between operations  14.9 us (3%)
  local copies, waits for them, and re-layouts  11.6 us (2%)
  other arithmetic  7.21 us (1%)
    all_to_all x3, blocking collectives, per_device(): jax.lax.all_to_all(e_next, axis_name='tensor', split_axis=0, concat_axis=0)  153 us
    all_gather x3, waiting for transfers between devices, per_device(): full_rows = lax.all_gather(iterate, 'tensor', axis=0, tiled=True)  151 us
    all_to_all x1, blocking collectives, per_device(): lax.all_to_all(direction, 'shard', split_axis=0, concat_axis=0, tiled=True)  41.5 us
    all_to_all x1, blocking collectives, per_device(): lax.all_to_all(result, 'shard', split_axis=0, concat_axis=0, tiled=True)  40.3 us
    dot_general x6, matrix products, product(): jnp.einsum('ij,jl->il', left, right, precision=lax.Precision.HIGHEST, pre...  24.6 us
    all_to_all x1, blocking collectives, per_device(): lax.all_to_all(by_owner, 'tensor', split_axis=1, concat_axis=2, tiled=True)  18.7 us
    dot_general x3, matrix products, against(): jnp.einsum('ij,lj->il', left, right, precision=lax.Precision.HIGHEST, pre...  17.8 us
    all_to_all x1, blocking collectives, per_device(): lax.all_to_all(lax.all_to_all(result, 'shard', split_axis=0, concat_axis=...  17.4 us
  transfers between devices with their start and end apart: 3, of which 3 were waited for; matrix products, arithmetic and copies ran while one was open for 0% of the time, Pallas kernels for 0%

profile of v1, /device:TPU:1, one launch (start us, length us, event | category | flops | bytes accessed | tf_op | source)
XLA Modules:
  0.0 505.4 jit_solution(17944522268057107197)
XLA Ops:
  7.2 0.0 all-gather.4.cloned.1.call-start
  7.2 2.6 convert_add_fusion
  9.8 41.5 %all_to_all.52 = f32[64,16,256]{2,1,0:T(8,128)S(1)} all-to-all(f32[64,16,256]{2,1,0:T(8,128)S(1)} %get-tuple-element.4), channel_id=1, replica_groups=mesh['shard'=64,'tensor'=4] {'shard'}, dimensions={0} | all-to-all | bytes 2097152 | tf_op jit(solution)/shard_map/all_to_all | solution.py:40
  51.2 0.6 copy.12
  51.8 18.7 %all_to_all.53 = f32[64,16,256]{2,0,1:T(8,128)S(1)} all-to-all(f32[64,16,256]{2,0,1:T(8,128)S(1)} %copy.12), channel_id=1, replica_groups=mesh['shard'=64,'tensor'=4] {'tensor'}, dimensions={1} | all-to-all | bytes 2097152 | tf_op jit(solution)/shard_map/all_to_all | solution.py:41
  70.5 0.9 multiply_reduce_fusion
  71.4 7.6 %psum.7 = f32[]{:T(128)} all-reduce(f32[]{:T(128)} %multiply_reduce_fusion), channel_id=1, replica_groups=mesh['shard'=64,'tensor'=4] {'tensor'}, use_global_device_ids=true, to_apply=%region_1.0 | all-reduce | flops 1 | bytes 8 | tf_op jit(solution)/shard_map/psum | solution.py:46
  79.6 0.1 broadcast_divide_fusion
  79.7 0.7 copy.13
  80.4 1.2 copy.16
  81.6 0.0 all-gather.4.cloned.1.call-update
  81.6 0.0 all-gather.6.cloned.1.call-start
  81.6 47.9 %all-gather.4.cloned.1.call-done = f32[1024,1024]{1,0:T(8,128)} async-done(((f32[256,1024]{1,0:T(8,128)}), f32[1024,1024]{1,0:T(8,128)}) %all-gather.4.cloned.1.call-update) | async-done | bytes 4194320 | tf_op jit(solution)/shard_map/all_gather | solution.py:49
  129.6 5.9 %fusion.4 = f32[256,1024]{1,0:T(8,128)S(1)} fusion(f32[256,1024]{1,0:T(8,128)} %bitcast.35, f32[1024,1024]{1,0:T(8,128)} %all-gather.4.cloned.1.call-done), kind=kOutput, calls=%fused_computation.14 | convolution fusion | flops 3221225472 | bytes 6291456 | tf_op jit(solution)/shard_map/ij,lj->il/dot_general | solution.py:27
  135.5 0.5 stack.6
  136.1 50.9 %all_to_all.54 = f32[4,256,1024]{2,1,0:T(8,128)S(1)} all-to-all(f32[4,256,1024]{2,1,0:T(8,128)S(1)} %stack.6), channel_id=1, replica_groups=mesh['shard'=64,'tensor'=4] {'tensor'}, dimensions={0} | all-to-all | bytes 8388608 | tf_op jit(solution)/shard_map/all_to_all | solution.py:53
  187.0 0.0 copy-start
  187.0 0.0 copy-start.5
  187.0 3.8 fusion.3
  190.8 0.0 copy-done
  190.8 0.0 copy-done.5
  190.8 4.7 convolution_add_fusion.2
  195.5 0.0 all-gather.6.cloned.1.call-update
  195.5 0.0 all-gather.8.cloned.1.call-start
  195.6 51.5 %all-gather.6.cloned.1.call-done = f32[1024,1024]{1,0:T(8,128)} async-done(((f32[256,1024]{1,0:T(8,128)}), f32[1024,1024]{1,0:T(8,128)}) %all-gather.6.cloned.1.call-update) | async-done | bytes 4194320 | tf_op jit(solution)/shard_map/all_gather | solution.py:49
  247.0 5.9 %fusion.5 = f32[256,1024]{1,0:T(8,128)S(1)} fusion(f32[256,1024]{1,0:T(8,128)} %convolution_add_fusion.2, f32[1024,1024]{1,0:T(8,128)} %all-gather.6.cloned.1.call-done), kind=kOutput, calls=%fused_computation.15 | convolution fusion | flops 3221225472 | bytes 6291456 | tf_op jit(solution)/shard_map/ij,lj->il/dot_general | solution.py:27
  253.0 0.5 stack.7
  253.5 51.1 %all_to_all.55 = f32[4,256,1024]{2,1,0:T(8,128)S(1)} all-to-all(f32[4,256,1024]{2,1,0:T(8,128)S(1)} %stack.7), channel_id=1, replica_groups=mesh['shard'=64,'tensor'=4] {'tensor'}, dimensions={0} | all-to-all | bytes 8388608 | tf_op jit(solution)/shard_map/all_to_all | solution.py:53
  304.7 0.0 copy-start.1
  304.7 0.0 copy-start.3
  304.7 3.8 fusion.2
  308.5 0.0 copy-done.1
  308.5 0.0 copy-done.3
  308.5 4.7 convolution_add_fusion.1
  313.2 0.0 all-gather.8.cloned.1.call-update
  313.2 51.5 %all-gather.8.cloned.1.call-done = f32[1024,1024]{1,0:T(8,128)} async-done(((f32[256,1024]{1,0:T(8,128)}), f32[1024,1024]{1,0:T(8,128)}) %all-gather.8.cloned.1.call-update) | async-done | bytes 4194320 | tf_op jit(solution)/shard_map/all_gather | solution.py:49
  364.8 5.9 %fusion.6 = f32[256,1024]{1,0:T(8,128)S(1)} fusion(f32[256,1024]{1,0:T(8,128)} %convolution_add_fusion.1, f32[1024,1024]{1,0:T(8,128)} %all-gather.8.cloned.1.call-done), kind=kOutput, calls=%fused_computation.16 | convolution fusion | flops 3221225472 | bytes 6291456 | tf_op jit(solution)/shard_map/ij,lj->il/dot_general | solution.py:27
  370.7 0.5 stack.8
  371.2 50.8 %all_to_all.56 = f32[4,256,1024]{2,1,0:T(8,128)S(1)} all-to-all(f32[4,256,1024]{2,1,0:T(8,128)S(1)} %stack.8), channel_id=1, replica_groups=mesh['shard'=64,'tensor'=4] {'tensor'}, dimensions={0} | all-to-all | bytes 8388608 | tf_op jit(solution)/shard_map/all_to_all | solution.py:53
  422.0 0.0 copy-start.2
  422.0 0.0 copy-start.4
  422.0 3.8 fusion.1
  425.8 0.0 copy-done.2
  425.8 0.0 copy-done.4
  425.9 3.8 fusion
  429.6 0.3 reshape.32
  430.0 40.3 %all_to_all.57 = f32[64,4,1024]{2,1,0:T(4,128)S(1)} all-to-all(f32[64,4,1024]{2,1,0:T(4,128)S(1)} %reshape.32), channel_id=1, replica_groups=mesh['shard'=64,'tensor'=4] {'shard'}, dimensions={0} | all-to-all | bytes 2097152 | tf_op jit(solution)/shard_map/all_to_all | solution.py:60
  470.3 0.9 copy.14
  471.2 2.0 reshape.33
  473.2 17.4 %all_to_all.58 = f32[4,1,65536]{2,1,0:T(1,128)S(1)} all-to-all(f32[4,1,65536]{2,1,0:T(1,128)S(1)} %reshape.33), channel_id=1, replica_groups=mesh['shard'=64,'tensor'=4] {'tensor'}, dimensions={0} | all-to-all | bytes 2097152 | tf_op jit(solution)/shard_map/all_to_all | solution.py:59
  490.7 0.5 broadcast.40
  491.2 3.7 reduce.3
  494.9 1.4 reshape.34
  496.3 1.0 copy.15
  497.4 1.3 all_to_all.44
Async XLA Ops:
  7.2 122.4 %all-gather.4.cloned.1.call-start = ((), (), s32[]{:S(2)}) async-start(), calls=%async_computation.7 | async-start | bytes 5242880 | tf_op jit(solution)/shard_map/all_gather | solution.py:49
  81.6 165.4 %all-gather.6.cloned.1.call-start = ((), (), s32[]{:S(2)}) async-start(), calls=%async_computation.8 | async-start | bytes 5242880 | tf_op jit(solution)/shard_map/all_gather | solution.py:49
  187.0 3.8 copy-start
  187.0 3.8 copy-start.5
  195.5 169.2 %all-gather.8.cloned.1.call-start = ((), (), s32[]{:S(2)}) async-start(), calls=%async_computation.9 | async-start | bytes 5242880 | tf_op jit(solution)/shard_map/all_gather | solution.py:49
  304.7 3.8 copy-start.1
  304.7 3.8 copy-start.3
  422.0 3.8 copy-start.2
  422.0 3.8 copy-start.4
Sparse Core Ops, SparseCore 0:
  81.7 47.8 all-gather.3
  195.7 51.3 all-gather.5
  313.4 51.3 all-gather.7
